TPU v7x, 32 devices: a whole 2x2x4 slice. The times are simulated.
32 devices in a mesh: shard: 4 (over z), tensor: 2 (over core), section: 4 (over y, x).
Axes of the slice: x: 2, y: 2, z: 4, core: 2. Of those that a mesh axis runs over, the one named last changes fastest.
Arguments:
- gradient: bfloat16 [2560, 2560], P('shard', ('tensor', 'section')), may hold values from -100 to 100
- gain_grad: float32 [2, 2560], P(None, 'shard'), may hold values from -12 to 12
- left_statistic: float32 [2560, 2560], P('shard', ('tensor', 'section')), may hold values from -1 to 3, as said below
- left_basis: float32 [2560, 2560], P('shard', ('tensor', 'section')), may hold values from -1 to 1.5
- first_moment: float32 [2560, 2560], P('shard', ('tensor', 'section')), may hold values from -3 to 3
- second_moment: float32 [2560, 2560], P('shard', ('tensor', 'section')), may hold values from 0.2 to 2
- norm_gains: float32 [2, 2560], P(None, 'shard'), may hold values from 0.5 to 1.5
- gain_first: float32 [2, 2560], P(None, 'shard'), may hold values from -2 to 2
- gain_second: float32 [2, 2560], P(None, 'shard'), may hold values from 0.5 to 5
Outputs:
- update: float32 [2560, 2560], P('shard', ('tensor', 'section'))
- new_first: float32 [2560, 2560], P('shard', ('tensor', 'section'))
- new_second: float32 [2560, 2560], P('shard', ('tensor', 'section'))
- new_statistic: float32 [2560, 2560], P('shard', ('tensor', 'section'))
- new_basis: float32 [2560, 2560], P('shard', ('tensor', 'section'))
- new_gains: float32 [2, 2560], P(None, 'shard')
- new_gain_first: float32 [2, 2560], P(None, 'shard')
- new_gain_second: float32 [2, 2560], P(None, 'shard')
Inputs may be any that keep to these rules, and one draw needn't show every extreme that they name: `left_statistic`: symmetric.
All inputs are finite; a program needn't handle non-finite values.
Results may differ from a plain program's by a relative error of at most 0.0003.
Values may be sent and summed in bfloat16 or wider, within the bound.
A program may use at most 128 MiB of HBM per device.

v0:
```python
import jax
import jax.numpy as jnp
from jax import lax
from jax.sharding import PartitionSpec as P

D = 2560
NS_STEPS = 3


def matmul(left_side, right_side):
    return jnp.dot(
        left_side, right_side, precision=lax.Precision.HIGHEST, preferred_element_type=jnp.float32
    )


def times_rows(full_rows, segment):
    return matmul(full_rows, segment)


def transposed_terms(full_rows, local_block):
    return matmul(full_rows.T, local_block)


def row_panel(local_block):
    return lax.all_gather(local_block, ("tensor", "section"), axis=1, tiled=True)


def on_device(
    gradient,
    gain_grad,
    left_statistic,
    left_basis,
    first_moment,
    second_moment,
    norm_gains,
    gain_first,
    gain_second,
):
    group_size = lax.axis_size(("tensor", "section"))
    grad_float = gradient.astype(jnp.float32)
    local_sum = jnp.sum(grad_float * grad_float) + jnp.sum(gain_grad * gain_grad) / group_size
    squares_total = lax.psum(local_sum, ("shard", "tensor", "section"))
    clip_factor = jnp.minimum(1.0, D / jnp.sqrt(squares_total + 1e-06))
    clipped = clip_factor * grad_float
    rotate_scale = 1.0
    outer_scale = 1.0
    basis_rows = row_panel(left_basis)
    rotated = rotate_scale * lax.psum_scatter(
        transposed_terms(basis_rows, clipped), "shard", scatter_dimension=0, tiled=True
    )
    partner = clip_factor * lax.all_gather(gradient, "shard", axis=0, tiled=True).astype(
        jnp.float32
    )
    outer_rows = matmul(clipped, partner.T)
    outer_part = lax.psum_scatter(
        outer_rows, ("tensor", "section"), scatter_dimension=1, tiled=True
    )
    new_statistic = 0.95 * left_statistic + 0.05 / D * (outer_scale * outer_part)
    new_first = 0.9 * first_moment + 0.1 * rotated
    new_second = 0.95 * second_moment + 0.05 * rotated * rotated
    direction = new_first / (jnp.sqrt(new_second) + 1e-08)
    update = times_rows(basis_rows, lax.all_gather(direction, "shard", axis=0, tiled=True))
    statistic_rows = row_panel(new_statistic)
    power_product = times_rows(
        statistic_rows, lax.all_gather(left_basis, "shard", axis=0, tiled=True)
    )
    power_sum = lax.psum(jnp.sum(power_product * power_product), ("shard", "tensor", "section"))
    iterate = 0.9 * jnp.sqrt(D / (power_sum + 1e-06)) * power_product
    for sweep_index in range(NS_STEPS):
        iterate_rows = row_panel(iterate)
        gram_block = lax.psum_scatter(
            transposed_terms(iterate_rows, iterate), "shard", scatter_dimension=0, tiled=True
        )
        applied = times_rows(iterate_rows, lax.all_gather(gram_block, "shard", axis=0, tiled=True))
        iterate = 1.5 * iterate - 0.5 * applied
    gain_clipped = clip_factor * gain_grad
    new_gain_first = 0.9 * gain_first + 0.1 * gain_clipped
    new_gain_second = 0.95 * gain_second + 0.05 * gain_clipped * gain_clipped
    new_gains = norm_gains - 0.01 * new_gain_first / (jnp.sqrt(new_gain_second) + 1e-08)
    return (
        update,
        new_first,
        new_second,
        new_statistic,
        iterate,
        new_gains,
        new_gain_first,
        new_gain_second,
    )


def solution(mesh):
    return jax.shard_map(
        on_device,
        mesh=mesh,
        in_specs=(
            P("shard", ("tensor", "section")),
            P(None, "shard"),
            P("shard", ("tensor", "section")),
            P("shard", ("tensor", "section")),
            P("shard", ("tensor", "section")),
            P("shard", ("tensor", "section")),
            P(None, "shard"),
            P(None, "shard"),
            P(None, "shard"),
        ),
        out_specs=(
            P("shard", ("tensor", "section")),
            P("shard", ("tensor", "section")),
            P("shard", ("tensor", "section")),
            P("shard", ("tensor", "section")),
            P("shard", ("tensor", "section")),
            P(None, "shard"),
            P(None, "shard"),
            P(None, "shard"),
        ),
        check_vma=False,
    )
```

profile of v0, /device:TPU:0, one launch (start us, length us, event | category | flops | bytes accessed | tf_op | source)
XLA Modules:
  0.0 1141.1 jit_solution(16108901470709755)
XLA Ops:
  7.2 0.0 all-gather.16.cloned.1.call-start
  7.2 0.7 all-gather.16.cloned.1.call-update
  7.9 0.0 reduce-scatter.8.cloned.1.call-start
  7.9 1.3 multiply_reduce_fusion.1
  9.9 1.8 fusion.7
  12.4 43.9 %psum.14 = f32[]{:T(128)} all-reduce(f32[]{:T(128)S(6)} %add.50), channel_id=1, replica_groups=mesh['shard'=4,'tensor'=2,'section'=4] {'shard','tensor','section'}, use_global_device_ids=true, to_apply=%region_2.0 | all-reduce | flops 1 | bytes 8 | tf_op jit(solution)/shard_map/psum | solution.py:42
  57.0 0.0 all-gather.16.cloned.1.call-done
  57.0 14.8 %fusion = f32[640,2560]{0,1:T(8,128)} fusion(bf16[2560,320]{0,1:T(8,128)(2,1)} %all-gather.16.cloned.1.call-done, f32[]{:T(128)S(6)} %min.3, bf16[640,320]{0,1:T(8,128)(2,1)} %param.9), kind=kOutput, calls=%fused_computation.1 | convolution fusion | flops 6293504000 | bytes 8601604 | tf_op jit(solution)/shard_map/dot_general | solution.py:11
  71.9 0.0 all-gather.20.cloned.1.call-start
  71.9 0.7 all-gather.20.cloned.1.call-update
  72.6 0.0 all-gather.18.cloned.1.call-start
  72.7 62.8 %reduce-scatter.8.cloned.1.call-done = f32[640,320]{0,1:T(8,128)} async-done(((f32[640,2560]{0,1:T(8,128)}), f32[640,320]{0,1:T(8,128)}) %reduce-scatter.8.cloned.1.call-update) | async-done | bytes 819216 | tf_op jit(solution)/shard_map/reduce_scatter | solution.py:55
  135.4 2.2 multiply_add_fusion
  137.6 0.0 all-gather.18.cloned.1.call-update
  137.6 0.2 all-gather.22.cloned.1.call-start
  137.8 64.9 %all-gather.20.cloned.1.call-done = f32[2560,320]{0,1:T(8,128)} async-done(((f32[640,320]{0,1:T(8,128)}), f32[2560,320]{0,1:T(8,128)}) %all-gather.20.cloned.1.call-update) | async-done | bytes 3276816 | tf_op jit(solution)/shard_map/all_gather | solution.py:65
  202.7 47.8 %all-gather.18.cloned.1.call-done = f32[640,2560]{0,1:T(8,128)} async-done(((f32[640,320]{0,1:T(8,128)}), f32[640,2560]{0,1:T(8,128)}) %all-gather.18.cloned.1.call-update) | async-done | bytes 6553616 | tf_op jit(solution)/shard_map/all_gather | solution.py:25
  250.5 11.6 %multiply_reduce_fusion = (f32[]{:T(128)}, f32[640,320]{0,1:T(8,128)S(1)}) fusion(f32[640,2560]{0,1:T(8,128)} %all-gather.18.cloned.1.call-done, f32[2560,320]{0,1:T(8,128)} %all-gather.20.cloned.1.call-done), kind=kOutput, calls=%fused_computation.17 | convolution fusion | flops 6291865600 | bytes 10649604 | tf_op jit(solution)/shard_map/dot_general | solution.py:11
  262.2 39.5 %psum.15 = f32[]{:T(128)} all-reduce(f32[]{:T(128)} %get-tuple-element.14), channel_id=1, replica_groups=mesh['shard'=4,'tensor'=2,'section'=4] {'shard','tensor','section'}, use_global_device_ids=true, to_apply=%region_6.0 | all-reduce | flops 1 | bytes 8 | tf_op jit(solution)/shard_map/psum | solution.py:67
  302.4 0.9 broadcast_multiply_fusion
  303.4 0.0 all-gather.22.cloned.1.call-update
  303.4 0.0 reduce-scatter.10.cloned.1.call-start
  303.4 47.7 %all-gather.22.cloned.1.call-done = f32[640,2560]{0,1:T(8,128)} async-done(((f32[640,320]{0,1:T(8,128)}), f32[640,2560]{0,1:T(8,128)}) %all-gather.22.cloned.1.call-update) | async-done | bytes 6553616 | tf_op jit(solution)/shard_map/all_gather | solution.py:25
  351.1 15.1 %fusion.14 = f32[2560,320]{1,0:T(8,128)} fusion(f32[640,2560]{0,1:T(8,128)} %all-gather.22.cloned.1.call-done, f32[640,320]{0,1:T(8,128)} %broadcast_multiply_fusion), kind=kOutput, calls=%fused_computation.29 | convolution fusion | flops 6291456000 | bytes 10649600 | tf_op jit(solution)/shard_map/dot_general | solution.py:11
  366.2 0.0 reduce-scatter.10.cloned.1.call-update
  366.2 0.0 all-gather.24.cloned.1.call-start
  366.3 72.8 %reduce-scatter.10.cloned.1.call-done = f32[640,320]{1,0:T(8,128)} async-done(((f32[2560,320]{1,0:T(8,128)}), f32[640,320]{1,0:T(8,128)}) %reduce-scatter.10.cloned.1.call-update) | async-done | bytes 819216 | tf_op jit(solution)/shard_map/reduce_scatter | solution.py:71
  439.1 0.0 all-gather.24.cloned.1.call-update
  439.1 0.3 all-gather.26.cloned.1.call-start
  439.4 78.2 %all-gather.24.cloned.1.call-done = f32[2560,320]{1,0:T(8,128)} async-done(((f32[640,320]{1,0:T(8,128)}), f32[2560,320]{1,0:T(8,128)}) %all-gather.24.cloned.1.call-update) | async-done | bytes 3276816 | tf_op jit(solution)/shard_map/all_gather | solution.py:74
  517.6 12.1 %fusion.4 = f32[640,320]{0,1:T(8,128)} fusion(f32[640,2560]{0,1:T(8,128)} %all-gather.22.cloned.1.call-done, f32[2560,320]{1,0:T(8,128)} %all-gather.24.cloned.1.call-done, f32[640,320]{0,1:T(8,128)S(1)} %copy-done.2), kind=kOutput, calls=%fused_computation.9 | convolution fusion | flops 6292070400 | bytes 11468800 | tf_op jit(solution)/shard_map/dot_general | solution.py:11
  529.7 0.0 reduce-scatter.12.cloned.1.call-start
  529.7 45.3 %all-gather.26.cloned.1.call-done = f32[640,2560]{0,1:T(8,128)} async-done(((f32[640,320]{0,1:T(8,128)}), f32[640,2560]{0,1:T(8,128)}) %all-gather.26.cloned.1.call-update) | async-done | bytes 6553616 | tf_op jit(solution)/shard_map/all_gather | solution.py:25
  575.0 15.1 %fusion.15 = f32[2560,320]{1,0:T(8,128)} fusion(f32[640,2560]{0,1:T(8,128)} %all-gather.26.cloned.1.call-done, f32[640,320]{0,1:T(8,128)} %fusion.4), kind=kOutput, calls=%fused_computation.30 | convolution fusion | flops 6291456000 | bytes 10649600 | tf_op jit(solution)/shard_map/dot_general | solution.py:11
  590.1 0.0 reduce-scatter.12.cloned.1.call-update
  590.1 0.0 all-gather.28.cloned.1.call-start
  590.2 72.8 %reduce-scatter.12.cloned.1.call-done = f32[640,320]{1,0:T(8,128)} async-done(((f32[2560,320]{1,0:T(8,128)}), f32[640,320]{1,0:T(8,128)}) %reduce-scatter.12.cloned.1.call-update) | async-done | bytes 819216 | tf_op jit(solution)/shard_map/reduce_scatter | solution.py:71
  663.0 0.0 all-gather.28.cloned.1.call-update
  663.0 0.0 all-gather.12.cloned.1.call-start
  663.1 0.7 all-gather.12.cloned.1.call-update
  663.8 0.4 all-gather.30.cloned.1.call-start
  664.2 77.1 %all-gather.28.cloned.1.call-done = f32[2560,320]{1,0:T(8,128)} async-done(((f32[640,320]{1,0:T(8,128)}), f32[2560,320]{1,0:T(8,128)}) %all-gather.28.cloned.1.call-update) | async-done | bytes 3276816 | tf_op jit(solution)/shard_map/all_gather | solution.py:74
  741.3 12.1 %fusion.5 = f32[640,320]{0,1:T(8,128)} fusion(f32[640,2560]{0,1:T(8,128)} %all-gather.26.cloned.1.call-done, f32[2560,320]{1,0:T(8,128)} %all-gather.28.cloned.1.call-done, f32[640,320]{0,1:T(8,128)S(1)} %copy-done.1), kind=kOutput, calls=%fused_computation.10 | convolution fusion | flops 6292070400 | bytes 11468800 | tf_op jit(solution)/shard_map/dot_general | solution.py:11
  753.4 0.0 all-gather.30.cloned.1.call-update
  753.4 0.0 reduce-scatter.6.cloned.1.call-start
  753.5 35.1 %all-gather.12.cloned.1.call-done = f32[640,2560]{0,1:T(8,128)} async-done(((f32[640,320]{0,1:T(8,128)}), f32[640,2560]{0,1:T(8,128)}) %all-gather.12.cloned.1.call-update) | async-done | bytes 6553616 | tf_op jit(solution)/shard_map/all_gather | solution.py:25
  788.6 11.4 convolution_bitcast_fusion
  800.0 0.0 reduce-scatter.6.cloned.1.call-update
  800.0 0.2 reduce-scatter.14.cloned.1.call-start
  800.2 37.5 %all-gather.30.cloned.1.call-done = f32[640,2560]{0,1:T(8,128)} async-done(((f32[640,320]{0,1:T(8,128)}), f32[640,2560]{0,1:T(8,128)}) %all-gather.30.cloned.1.call-update) | async-done | bytes 6553616 | tf_op jit(solution)/shard_map/all_gather | solution.py:25
  837.7 14.8 %fusion.16 = f32[2560,320]{1,0:T(8,128)} fusion(f32[640,2560]{0,1:T(8,128)} %all-gather.30.cloned.1.call-done, f32[640,320]{0,1:T(8,128)S(1)} %copy-done), kind=kOutput, calls=%fused_computation.31 | convolution fusion | flops 6291456000 | bytes 10649600 | tf_op jit(solution)/shard_map/dot_general | solution.py:11
  852.6 0.0 reduce-scatter.14.cloned.1.call-update
  852.6 0.0 all-gather.14.cloned.1.call-start
  852.7 49.8 %reduce-scatter.6.cloned.1.call-done = f32[640,320]{0,1:T(8,128)} async-done(((f32[2560,320]{0,1:T(8,128)}), f32[640,320]{0,1:T(8,128)}) %reduce-scatter.6.cloned.1.call-update) | async-done | bytes 819216 | tf_op jit(solution)/shard_map/reduce_scatter | solution.py:48
  902.5 2.8 add_divide_fusion
  905.3 0.0 all-gather.14.cloned.1.call-update
  905.3 0.3 all-gather.32.cloned.1.call-start
  905.5 72.0 %reduce-scatter.14.cloned.1.call-done = f32[640,320]{1,0:T(8,128)} async-done(((f32[2560,320]{1,0:T(8,128)}), f32[640,320]{1,0:T(8,128)}) %reduce-scatter.14.cloned.1.call-update) | async-done | bytes 819216 | tf_op jit(solution)/shard_map/reduce_scatter | solution.py:71
  977.6 0.0 all-gather.32.cloned.1.call-update
  977.6 0.6 divide_subtract_fusion
  978.3 67.4 %all-gather.14.cloned.1.call-done = f32[2560,320]{0,1:T(8,128)} async-done(((f32[640,320]{0,1:T(8,128)}), f32[2560,320]{0,1:T(8,128)}) %all-gather.14.cloned.1.call-update) | async-done | bytes 3276816 | tf_op jit(solution)/shard_map/all_gather | solution.py:62
  1045.7 11.7 %convolution_bitcast_fusion.1 = f32[640,320]{0,1:T(8,128)} fusion(f32[2560,320]{0,1:T(8,128)} %all-gather.14.cloned.1.call-done, f32[640,2560]{0,1:T(8,128)} %all-gather.12.cloned.1.call-done), kind=kOutput, calls=%fused_computation.5 | convolution fusion | flops 6291456000 | bytes 10649600 | tf_op jit(solution)/shard_map/dot_general | solution.py:11
  1057.4 64.9 %all-gather.32.cloned.1.call-done = f32[2560,320]{1,0:T(8,128)} async-done(((f32[640,320]{1,0:T(8,128)}), f32[2560,320]{1,0:T(8,128)}) %all-gather.32.cloned.1.call-update) | async-done | bytes 3276816 | tf_op jit(solution)/shard_map/all_gather | solution.py:74
  1122.3 12.1 %fusion.6 = f32[640,320]{0,1:T(8,128)} fusion(f32[640,2560]{0,1:T(8,128)} %all-gather.30.cloned.1.call-done, f32[2560,320]{1,0:T(8,128)} %all-gather.32.cloned.1.call-done, f32[640,320]{0,1:T(8,128)S(1)} %copy-done), kind=kOutput, calls=%fused_computation.11 | convolution fusion | flops 6292070400 | bytes 11468800 | tf_op jit(solution)/shard_map/dot_general | solution.py:11
  (24 shorter events, 0.1 us)
Async XLA Ops:
  7.2 49.9 %all-gather.16.cloned.1.call-start = ((), (), s32[]{:S(2)}) async-start(), calls=%async_computation.8 | async-start | bytes 2048000 | tf_op jit(solution)/shard_map/all_gather | solution.py:51
  7.9 127.5 %reduce-scatter.8.cloned.1.call-start = ((), (), s32[]{:S(2)}) async-start(), calls=%async_computation.9 | async-start | bytes 7372800 | tf_op jit(solution)/shard_map/reduce_scatter | solution.py:55
  71.8 63.6 %copy-start.6 = (f32[640,320]{0,1:T(8,128)S(1)}, f32[640,320]{0,1:T(8,128)}, u32[]{:S(2)}) copy-start(f32[640,320]{0,1:T(8,128)} %param.11) | copy-start | bytes 2457604
  71.9 130.8 %all-gather.20.cloned.1.call-start = ((), (), s32[]{:S(2)}) async-start(), calls=%async_computation.11 | async-start | bytes 4096000 | tf_op jit(solution)/shard_map/all_gather | solution.py:65
  72.6 177.9 %all-gather.18.cloned.1.call-start = ((), (), s32[]{:S(2)}) async-start(), calls=%async_computation.10 | async-start | bytes 7372800 | tf_op jit(solution)/shard_map/all_gather | solution.py:25
  137.6 213.5 %all-gather.22.cloned.1.call-start = ((), (), s32[]{:S(2)}) async-start(), calls=%async_computation.12 | async-start | bytes 7372800 | tf_op jit(solution)/shard_map/all_gather | solution.py:25
  303.4 135.7 %reduce-scatter.10.cloned.1.call-start = ((), (), s32[]{:S(2)}) async-start(), calls=%async_computation.13 | async-start | bytes 4915200 | tf_op jit(solution)/shard_map/reduce_scatter | solution.py:71
  366.2 151.4 %copy-start.2 = (f32[640,320]{0,1:T(8,128)S(1)}, f32[640,320]{0,1:T(8,128)}, u32[]{:S(2)}) copy-start(f32[640,320]{0,1:T(8,128)} %broadcast_multiply_fusion) | copy-start | bytes 2457604
  366.2 151.3 %all-gather.24.cloned.1.call-start = ((), (), s32[]{:S(2)}) async-start(), calls=%async_computation.14 | async-start | bytes 4915200 | tf_op jit(solution)/shard_map/all_gather | solution.py:74
  439.1 135.9 %all-gather.26.cloned.1.call-start = ((), (), s32[]{:S(2)}) async-start(), calls=%async_computation.15 | async-start | bytes 7372800 | tf_op jit(solution)/shard_map/all_gather | solution.py:25
  529.7 133.3 %reduce-scatter.12.cloned.1.call-start = ((), (), s32[]{:S(2)}) async-start(), calls=%async_computation.16 | async-start | bytes 4915200 | tf_op jit(solution)/shard_map/reduce_scatter | solution.py:71
  590.1 151.2 %copy-start.1 = (f32[640,320]{0,1:T(8,128)S(1)}, f32[640,320]{0,1:T(8,128)}, u32[]{:S(2)}) copy-start(f32[640,320]{0,1:T(8,128)} %fusion.4) | copy-start | bytes 2457604
  590.1 151.2 %all-gather.28.cloned.1.call-start = ((), (), s32[]{:S(2)}) async-start(), calls=%async_computation.17 | async-start | bytes 4915200 | tf_op jit(solution)/shard_map/all_gather | solution.py:74
  663.0 125.6 %all-gather.12.cloned.1.call-start = ((), (), s32[]{:S(2)}) async-start(), calls=%async_computation.5 | async-start | bytes 7372800 | tf_op jit(solution)/shard_map/all_gather | solution.py:25
  663.7 124.9 %copy-start.3 = (bf16[640,320]{0,1:T(8,128)(2,1)S(1)}, bf16[640,320]{0,1:T(8,128)(2,1)}, u32[]{:S(2)}) copy-start(bf16[640,320]{0,1:T(8,128)(2,1)} %param.9) | copy-start | bytes 1228804
  663.8 174.0 %all-gather.30.cloned.1.call-start = ((), (), s32[]{:S(2)}) async-start(), calls=%async_computation.18 | async-start | bytes 7372800 | tf_op jit(solution)/shard_map/all_gather | solution.py:25
  753.4 84.3 %copy-start = (f32[640,320]{0,1:T(8,128)S(1)}, f32[640,320]{0,1:T(8,128)}, u32[]{:S(2)}) copy-start(f32[640,320]{0,1:T(8,128)} %fusion.5) | copy-start | bytes 2457604
  753.4 149.0 %reduce-scatter.6.cloned.1.call-start = ((), (), s32[]{:S(2)}) async-start(), calls=%async_computation.6 | async-start | bytes 4096000 | tf_op jit(solution)/shard_map/reduce_scatter | solution.py:48
  800.0 177.6 %reduce-scatter.14.cloned.1.call-start = ((), (), s32[]{:S(2)}) async-start(), calls=%async_computation.19 | async-start | bytes 4915200 | tf_op jit(solution)/shard_map/reduce_scatter | solution.py:71
  852.6 49.9 %copy-start.4 = (f32[640,320]{0,1:T(8,128)S(1)}, f32[640,320]{0,1:T(8,128)}, u32[]{:S(2)}) copy-start(f32[640,320]{0,1:T(8,128)} %param.14) | copy-start | bytes 2457604
  852.6 49.9 %copy-start.5 = (f32[640,320]{0,1:T(8,128)S(1)}, f32[640,320]{0,1:T(8,128)}, u32[]{:S(2)}) copy-start(f32[640,320]{0,1:T(8,128)} %param.13) | copy-start | bytes 2457604
  852.6 125.0 %copy-start.7 = (f32[2,640]{1,0:T(2,128)S(1)}, f32[2,640]{1,0:T(2,128)}, u32[]{:S(2)}) copy-start(f32[2,640]{1,0:T(2,128)} %param.10) | copy-start | bytes 15364
  852.6 125.0 %copy-start.8 = (f32[2,640]{1,0:T(2,128)S(1)}, f32[2,640]{1,0:T(2,128)}, u32[]{:S(2)}) copy-start(f32[2,640]{1,0:T(2,128)} %param.15) | copy-start | bytes 15364
  852.6 125.0 %copy-start.9 = (f32[2,640]{1,0:T(2,128)S(1)}, f32[2,640]{1,0:T(2,128)}, u32[]{:S(2)}) copy-start(f32[2,640]{1,0:T(2,128)} %param.16) | copy-start | bytes 15364
  852.6 125.0 %copy-start.10 = (f32[2,640]{1,0:T(2,128)S(1)}, f32[2,640]{1,0:T(2,128)}, u32[]{:S(2)}) copy-start(f32[2,640]{1,0:T(2,128)} %param.17) | copy-start | bytes 15364
  852.6 193.0 %all-gather.14.cloned.1.call-start = ((), (), s32[]{:S(2)}) async-start(), calls=%async_computation.7 | async-start | bytes 4096000 | tf_op jit(solution)/shard_map/all_gather | solution.py:62
  905.3 217.0 %all-gather.32.cloned.1.call-start = ((), (), s32[]{:S(2)}) async-start(), calls=%async_computation.20 | async-start | bytes 4915200 | tf_op jit(solution)/shard_map/all_gather | solution.py:74
Sparse Core Ops, SparseCore 0:
  9.6 41.7 all-gather.15
  72.0 63.3 reduce-scatter.7
  137.1 65.5 all-gather.19
  205.2 45.2 all-gather.17
  303.5 47.5 all-gather.21
  366.4 72.6 reduce-scatter.9
  440.7 76.7 all-gather.23
  529.8 45.1 all-gather.25
  590.3 72.6 reduce-scatter.11
  664.5 76.7 all-gather.27
  743.4 45.1 all-gather.11
  791.1 46.6 all-gather.29
  840.1 62.2 reduce-scatter.5
  904.7 72.7 reduce-scatter.13
  979.6 65.9 all-gather.13
  1047.2 75.0 all-gather.31
where the time goes:
time: 1150 us; the launch traced here: 1140 us
  waiting for transfers between devices  898 us (78%)
  matrix products  131 us (11%)
  blocking collectives  83.5 us (7%)
  between operations  17 us (1%)
    all_gather x3, waiting for transfers between devices, on_device(): lax.all_gather(gram_block, 'shard', axis=0, tiled=True)  220 us
    reduce_scatter x3, waiting for transfers between devices, on_device(): lax.psum_scatter(transposed_terms(iterate_rows, iterate), 'shard', scatte...  218 us
    all_gather x5, waiting for transfers between devices, row_panel(): lax.all_gather(local_block, ('tensor', 'section'), axis=1, tiled=True)  213 us
    dot_general x10, matrix products, matmul(): jnp.dot(left_side, right_side, precision=lax.Precision.HIGHEST, preferred...  131 us
    all_gather x1, waiting for transfers between devices, on_device(): lax.all_gather(direction, 'shard', axis=0, tiled=True)  67.4 us
    all_gather x1, waiting for transfers between devices, on_device(): lax.all_gather(left_basis, 'shard', axis=0, tiled=True)  64.9 us
    reduce_scatter x1, waiting for transfers between devices, on_device(): lax.psum_scatter(outer_rows, ('tensor', 'section'), scatter_dimension=1,...  62.8 us
    reduce_scatter x1, waiting for transfers between devices, on_device(): lax.psum_scatter(transposed_terms(basis_rows, clipped), 'shard', scatter_...  49.8 us
  transfers between devices with their start and end apart: 16, of which 15 were waited for; matrix products, arithmetic and copies ran while one was open for 5% of the time, Pallas kernels for 0%

commit v1 on v0

--- a/solution.py
+++ b/solution.py
@@ -5,6 +5,24 @@
 
 D = 2560
 NS_STEPS = 3
+
+
+def gather_around(value, axis, dim):
+    ways, here, step = (lax.axis_size(axis), lax.axis_index(axis), value.shape[dim])
+    dims = [n * ways if d == dim else n for d, n in enumerate(value.shape)]
+    full = lax.dynamic_update_slice_in_dim(
+        jnp.zeros(dims, value.dtype), value, here * step, axis=dim
+    )
+    going_up = going_down = value
+    for far in range(1, ways // 2 + 1):
+        going_up = lax.ppermute(going_up, axis, [(d, (d + 1) % ways) for d in range(ways)])
+        full = lax.dynamic_update_slice_in_dim(full, going_up, (here - far) % ways * step, axis=dim)
+        if 2 * far < ways:
+            going_down = lax.ppermute(going_down, axis, [(d, (d - 1) % ways) for d in range(ways)])
+            full = lax.dynamic_update_slice_in_dim(
+                full, going_down, (here + far) % ways * step, axis=dim
+            )
+    return full
 
 
 def matmul(left_side, right_side):
@@ -61,9 +79,7 @@
     direction = new_first / (jnp.sqrt(new_second) + 1e-08)
     update = times_rows(basis_rows, lax.all_gather(direction, "shard", axis=0, tiled=True))
     statistic_rows = row_panel(new_statistic)
-    power_product = times_rows(
-        statistic_rows, lax.all_gather(left_basis, "shard", axis=0, tiled=True)
-    )
+    power_product = times_rows(statistic_rows, gather_around(left_basis, "shard", 0))
     power_sum = lax.psum(jnp.sum(power_product * power_product), ("shard", "tensor", "section"))
     iterate = 0.9 * jnp.sqrt(D / (power_sum + 1e-06)) * power_product
     for sweep_index in range(NS_STEPS):

time: 1150 us -> 1090 us (0.948)
  waiting for transfers between devices: 898 us -> 834 us
    all_gather x1 -> x0, waiting for transfers between devices: 64.9 us -> none  [on_device(): lax.all_gather(left_basis, 'shard', axis=0, tiled=True)]
    all_gather x5, waiting for transfers between devices: 213 us -> 165 us  [row_panel(): lax.all_gather(local_block, ('tensor', 'section'), axis=1, tiled=True)]
    ppermute x0 -> x3, waiting for transfers between devices: none -> 48.5 us  [the longest x2 35.9 us: gather_around(): lax.ppermute(going_up, axis, [(d, (d + 1) % ways) for d in range(ways)])]
  transfers between devices with their start and end apart: 16 -> 18, of which waited for: 15 -> 16; matrix products, arithmetic and copies ran while one was open for 5% -> 6% of each run, Pallas kernels for 0% -> 0%
where the time goes in v1:
time: 1090 us
  waiting for transfers between devices  834 us (77%)
  matrix products  131 us (12%)
  blocking collectives  81.7 us (7%)
  between operations  17.1 us (2%)
    all_gather x3, waiting for transfers between devices, on_device(): lax.all_gather(gram_block, 'shard', axis=0, tiled=True)  221 us
    reduce_scatter x3, waiting for transfers between devices, on_device(): lax.psum_scatter(transposed_terms(iterate_rows, iterate), 'shard', scatte...  218 us
    all_gather x5, waiting for transfers between devices, row_panel(): lax.all_gather(local_block, ('tensor', 'section'), axis=1, tiled=True)  165 us
    dot_general x10, matrix products, matmul(): jnp.dot(left_side, right_side, precision=lax.Precision.HIGHEST, preferred...  131 us
    all_gather x1, waiting for transfers between devices, on_device(): lax.all_gather(direction, 'shard', axis=0, tiled=True)  67.4 us
    reduce_scatter x1, waiting for transfers between devices, on_device(): lax.psum_scatter(outer_rows, ('tensor', 'section'), scatter_dimension=1,...  63.5 us
    reduce_scatter x1, waiting for transfers between devices, on_device(): lax.psum_scatter(transposed_terms(basis_rows, clipped), 'shard', scatter_...  49.6 us
    psum x1, blocking collectives, on_device(): squares_total = lax.psum(local_sum, ('shard', 'tensor', 'section'))  43.9 us
  transfers between devices with their start and end apart: 18, of which 16 were waited for; matrix products, arithmetic and copies ran while one was open for 6% of the time, Pallas kernels for 0%

profile of v1, /device:TPU:0, one launch (start us, length us, event | category | flops | bytes accessed | tf_op | source)
XLA Modules:
  0.0 1086.6 jit_solution(8951941868853338600)
XLA Ops:
  7.2 0.0 all-gather.15.cloned.1.call-start
  7.2 0.7 all-gather.15.cloned.1.call-update
  7.9 0.0 reduce-scatter.8.cloned.1.call-start
  7.9 1.3 multiply_reduce_fusion.1
  9.9 1.8 fusion.6
  12.4 43.9 %psum.14 = f32[]{:T(128)} all-reduce(f32[]{:T(128)S(6)} %add.77), channel_id=1, replica_groups=mesh['shard'=4,'tensor'=2,'section'=4] {'shard','tensor','section'}, use_global_device_ids=true, to_apply=%region_2.0 | all-reduce | flops 1 | bytes 8 | tf_op jit(solution)/shard_map/psum | solution.py:60
  57.0 0.0 all-gather.15.cloned.1.call-done
  57.0 14.8 %fusion = f32[640,2560]{0,1:T(8,128)} fusion(bf16[2560,320]{0,1:T(8,128)(2,1)} %all-gather.15.cloned.1.call-done, f32[]{:T(128)S(6)} %min.3, bf16[640,320]{0,1:T(8,128)(2,1)} %param.9), kind=kOutput, calls=%fused_computation.1 | convolution fusion | flops 6293504000 | bytes 8601604 | tf_op jit(solution)/shard_map/dot_general | solution.py:29
  71.8 0.0 reduce-scatter.8.cloned.1.call-update
  71.9 0.0 all-gather.17.cloned.1.call-start
  71.9 63.5 %reduce-scatter.8.cloned.1.call-done = f32[640,320]{0,1:T(8,128)} async-done(((f32[640,2560]{0,1:T(8,128)}), f32[640,320]{0,1:T(8,128)}) %reduce-scatter.8.cloned.1.call-update) | async-done | bytes 819216 | tf_op jit(solution)/shard_map/reduce_scatter | solution.py:73
  135.5 2.2 multiply_add_fusion
  137.6 0.0 all-gather.17.cloned.1.call-update
  137.6 0.0 all-gather.19.cloned.1.call-start
  137.7 1.5 collective-permute-start
  139.2 2.3 collective-permute-start.1
  141.6 19.5 %collective-permute-done = f32[640,320]{0,1:T(8,128)} collective-permute-done((f32[640,320]{0,1:T(8,128)}, f32[640,320]{0,1:T(8,128)}, u32[]{:S(2)}, u32[]{:S(2)}) %collective-permute-start) | collective-permute-done | bytes 819232 | tf_op jit(solution)/shard_map/ppermute | solution.py:18
  161.0 0.5 collective-permute-start.2
  161.6 0.4 broadcast_in_dim.3
  162.0 1.2 constant_dynamic-update-slice_fusion.3
  163.2 1.5 constant_dynamic-update-slice_fusion.2
  164.7 12.6 %collective-permute-done.1 = f32[640,320]{0,1:T(8,128)} collective-permute-done((f32[640,320]{0,1:T(8,128)}, f32[640,320]{0,1:T(8,128)}, u32[]{:S(2)}, u32[]{:S(2)}) %collective-permute-start.1) | collective-permute-done | bytes 819232 | tf_op jit(solution)/shard_map/ppermute | solution.py:21
  177.4 1.2 constant_dynamic-update-slice_fusion.1
  178.6 16.4 %collective-permute-done.2 = f32[640,320]{0,1:T(8,128)} collective-permute-done((f32[640,320]{0,1:T(8,128)}, f32[640,320]{0,1:T(8,128)}, u32[]{:S(2)}, u32[]{:S(2)}) %collective-permute-start.2) | collective-permute-done | bytes 819232 | tf_op jit(solution)/shard_map/ppermute | solution.py:18
  195.0 1.2 constant_dynamic-update-slice_fusion
  196.2 0.0 all-gather.17.cloned.1.call-done
  196.3 12.1 %multiply_reduce_fusion = (f32[]{:T(128)}, f32[640,320]{0,1:T(8,128)}) fusion(f32[640,2560]{0,1:T(8,128)} %all-gather.17.cloned.1.call-done, f32[2560,320]{0,1:T(8,128)S(1)} %constant_dynamic-update-slice_fusion), kind=kOutput, calls=%fused_computation.17 | convolution fusion | flops 6291865600 | bytes 10649604 | tf_op jit(solution)/shard_map/dot_general | solution.py:29
  208.4 37.7 %psum.15 = f32[]{:T(128)} all-reduce(f32[]{:T(128)} %get-tuple-element.14), channel_id=1, replica_groups=mesh['shard'=4,'tensor'=2,'section'=4] {'shard','tensor','section'}, use_global_device_ids=true, to_apply=%region_6.7 | all-reduce | flops 1 | bytes 8 | tf_op jit(solution)/shard_map/psum | solution.py:83
  246.9 2.1 broadcast_multiply_fusion
  249.0 0.2 reduce-scatter.10.cloned.1.call-start
  249.2 47.4 %all-gather.19.cloned.1.call-done = f32[640,2560]{0,1:T(8,128)} async-done(((f32[640,320]{0,1:T(8,128)}), f32[640,2560]{0,1:T(8,128)}) %all-gather.19.cloned.1.call-update) | async-done | bytes 6553616 | tf_op jit(solution)/shard_map/all_gather | solution.py:43
  296.6 15.1 %fusion.13 = f32[2560,320]{1,0:T(8,128)} fusion(f32[640,2560]{0,1:T(8,128)} %all-gather.19.cloned.1.call-done, f32[640,320]{0,1:T(8,128)} %broadcast_multiply_fusion), kind=kOutput, calls=%fused_computation.33 | convolution fusion | flops 6291456000 | bytes 10649600 | tf_op jit(solution)/shard_map/dot_general | solution.py:29
  311.7 0.0 reduce-scatter.10.cloned.1.call-update
  311.7 0.0 all-gather.21.cloned.1.call-start
  311.8 72.8 %reduce-scatter.10.cloned.1.call-done = f32[640,320]{1,0:T(8,128)} async-done(((f32[2560,320]{1,0:T(8,128)}), f32[640,320]{1,0:T(8,128)}) %reduce-scatter.10.cloned.1.call-update) | async-done | bytes 819216 | tf_op jit(solution)/shard_map/reduce_scatter | solution.py:87
  384.6 0.0 all-gather.23.cloned.1.call-start
  384.6 78.3 %all-gather.21.cloned.1.call-done = f32[2560,320]{1,0:T(8,128)} async-done(((f32[640,320]{1,0:T(8,128)}), f32[2560,320]{1,0:T(8,128)}) %all-gather.21.cloned.1.call-update) | async-done | bytes 3276816 | tf_op jit(solution)/shard_map/all_gather | solution.py:90
  462.9 12.1 %multiply_subtract_fusion = f32[640,320]{0,1:T(8,128)} fusion(f32[640,320]{0,1:T(8,128)S(1)} %copy-done.2, f32[640,2560]{0,1:T(8,128)} %all-gather.19.cloned.1.call-done, f32[2560,320]{1,0:T(8,128)} %all-gather.21.cloned.1.call-done), kind=kOutput, calls=%fused_computation.16 | convolution fusion | flops 6292070400 | bytes 11468800 | tf_op jit(solution)/shard_map/dot_general | solution.py:29
  475.0 0.3 reduce-scatter.12.cloned.1.call-start
  475.3 45.1 %all-gather.23.cloned.1.call-done = f32[640,2560]{0,1:T(8,128)} async-done(((f32[640,320]{0,1:T(8,128)}), f32[640,2560]{0,1:T(8,128)}) %all-gather.23.cloned.1.call-update) | async-done | bytes 6553616 | tf_op jit(solution)/shard_map/all_gather | solution.py:43
  520.4 15.1 %fusion.14 = f32[2560,320]{1,0:T(8,128)} fusion(f32[640,2560]{0,1:T(8,128)} %all-gather.23.cloned.1.call-done, f32[640,320]{0,1:T(8,128)} %multiply_subtract_fusion), kind=kOutput, calls=%fused_computation.34 | convolution fusion | flops 6291456000 | bytes 10649600 | tf_op jit(solution)/shard_map/dot_general | solution.py:29
  535.5 0.0 all-gather.25.cloned.1.call-start
  535.5 72.8 %reduce-scatter.12.cloned.1.call-done = f32[640,320]{1,0:T(8,128)} async-done(((f32[2560,320]{1,0:T(8,128)}), f32[640,320]{1,0:T(8,128)}) %reduce-scatter.12.cloned.1.call-update) | async-done | bytes 819216 | tf_op jit(solution)/shard_map/reduce_scatter | solution.py:87
  608.3 0.0 all-gather.11.cloned.1.call-start
  608.4 0.5 all-gather.11.cloned.1.call-update
  608.9 0.0 all-gather.27.cloned.1.call-start
  609.0 77.8 %all-gather.25.cloned.1.call-done = f32[2560,320]{1,0:T(8,128)} async-done(((f32[640,320]{1,0:T(8,128)}), f32[2560,320]{1,0:T(8,128)}) %all-gather.25.cloned.1.call-update) | async-done | bytes 3276816 | tf_op jit(solution)/shard_map/all_gather | solution.py:90
  686.8 12.1 %fusion.4 = f32[640,320]{0,1:T(8,128)} fusion(f32[640,2560]{0,1:T(8,128)} %all-gather.23.cloned.1.call-done, f32[2560,320]{1,0:T(8,128)} %all-gather.25.cloned.1.call-done, f32[640,320]{0,1:T(8,128)S(1)} %copy-done.1), kind=kOutput, calls=%fused_computation.9 | convolution fusion | flops 6292070400 | bytes 11468800 | tf_op jit(solution)/shard_map/dot_general | solution.py:29
  698.9 0.4 reduce-scatter.6.cloned.1.call-start
  699.4 34.5 %all-gather.11.cloned.1.call-done = f32[640,2560]{0,1:T(8,128)} async-done(((f32[640,320]{0,1:T(8,128)}), f32[640,2560]{0,1:T(8,128)}) %all-gather.11.cloned.1.call-update) | async-done | bytes 6553616 | tf_op jit(solution)/shard_map/all_gather | solution.py:43
  733.9 11.4 %convolution_bitcast_fusion = f32[2560,320]{0,1:T(8,128)} fusion(f32[640,2560]{0,1:T(8,128)} %all-gather.11.cloned.1.call-done, bf16[640,320]{0,1:T(8,128)(2,1)S(1)} %copy-done.3, f32[]{:T(128)S(6)} %min.3), kind=kOutput, calls=%fused_computation | convolution fusion | flops 6291865600 | bytes 10240004 | tf_op jit(solution)/shard_map/dot_general | solution.py:29
  745.3 0.0 reduce-scatter.14.cloned.1.call-start
  745.4 37.8 %all-gather.27.cloned.1.call-done = f32[640,2560]{0,1:T(8,128)} async-done(((f32[640,320]{0,1:T(8,128)}), f32[640,2560]{0,1:T(8,128)}) %all-gather.27.cloned.1.call-update) | async-done | bytes 6553616 | tf_op jit(solution)/shard_map/all_gather | solution.py:43
  783.2 14.8 %fusion.15 = f32[2560,320]{1,0:T(8,128)} fusion(f32[640,2560]{0,1:T(8,128)} %all-gather.27.cloned.1.call-done, f32[640,320]{0,1:T(8,128)S(1)} %copy-done), kind=kOutput, calls=%fused_computation.35 | convolution fusion | flops 6291456000 | bytes 10649600 | tf_op jit(solution)/shard_map/dot_general | solution.py:29
  798.1 0.0 all-gather.13.cloned.1.call-start
  798.2 49.6 %reduce-scatter.6.cloned.1.call-done = f32[640,320]{0,1:T(8,128)} async-done(((f32[2560,320]{0,1:T(8,128)}), f32[640,320]{0,1:T(8,128)}) %reduce-scatter.6.cloned.1.call-update) | async-done | bytes 819216 | tf_op jit(solution)/shard_map/reduce_scatter | solution.py:66
  847.8 2.8 add_divide_fusion
  850.6 0.2 all-gather.29.cloned.1.call-start
  850.9 72.2 %reduce-scatter.14.cloned.1.call-done = f32[640,320]{1,0:T(8,128)} async-done(((f32[2560,320]{1,0:T(8,128)}), f32[640,320]{1,0:T(8,128)}) %reduce-scatter.14.cloned.1.call-update) | async-done | bytes 819216 | tf_op jit(solution)/shard_map/reduce_scatter | solution.py:87
  923.1 0.6 divide_subtract_fusion
  923.8 67.4 %all-gather.13.cloned.1.call-done = f32[2560,320]{0,1:T(8,128)} async-done(((f32[640,320]{0,1:T(8,128)}), f32[2560,320]{0,1:T(8,128)}) %all-gather.13.cloned.1.call-update) | async-done | bytes 3276816 | tf_op jit(solution)/shard_map/all_gather | solution.py:80
  991.2 11.7 %convolution_bitcast_fusion.1 = f32[640,320]{0,1:T(8,128)} fusion(f32[2560,320]{0,1:T(8,128)} %all-gather.13.cloned.1.call-done, f32[640,2560]{0,1:T(8,128)} %all-gather.11.cloned.1.call-done), kind=kOutput, calls=%fused_computation.5 | convolution fusion | flops 6291456000 | bytes 10649600 | tf_op jit(solution)/shard_map/dot_general | solution.py:29
  1002.9 64.9 %all-gather.29.cloned.1.call-done = f32[2560,320]{1,0:T(8,128)} async-done(((f32[640,320]{1,0:T(8,128)}), f32[2560,320]{1,0:T(8,128)}) %all-gather.29.cloned.1.call-update) | async-done | bytes 3276816 | tf_op jit(solution)/shard_map/all_gather | solution.py:90
  1067.8 12.1 %fusion.5 = f32[640,320]{0,1:T(8,128)} fusion(f32[640,2560]{0,1:T(8,128)} %all-gather.27.cloned.1.call-done, f32[2560,320]{1,0:T(8,128)} %all-gather.29.cloned.1.call-done, f32[640,320]{0,1:T(8,128)S(1)} %copy-done), kind=kOutput, calls=%fused_computation.10 | convolution fusion | flops 6292070400 | bytes 11468800 | tf_op jit(solution)/shard_map/dot_general | solution.py:29
  (32 shorter events, 0.2 us)
Async XLA Ops:
  7.2 49.9 %all-gather.15.cloned.1.call-start = ((), (), s32[]{:S(2)}) async-start(), calls=%async_computation.8 | async-start | bytes 2048000 | tf_op jit(solution)/shard_map/all_gather | solution.py:69
  7.9 127.6 %reduce-scatter.8.cloned.1.call-start = ((), (), s32[]{:S(2)}) async-start(), calls=%async_computation.9 | async-start | bytes 7372800 | tf_op jit(solution)/shard_map/reduce_scatter | solution.py:73
  71.8 63.6 %copy-start.6 = (f32[640,320]{0,1:T(8,128)S(1)}, f32[640,320]{0,1:T(8,128)}, u32[]{:S(2)}) copy-start(f32[640,320]{0,1:T(8,128)} %param.11) | copy-start | bytes 2457604
  71.9 124.4 %all-gather.17.cloned.1.call-start = ((), (), s32[]{:S(2)}) async-start(), calls=%async_computation.10 | async-start | bytes 7372800 | tf_op jit(solution)/shard_map/all_gather | solution.py:43
  137.6 159.0 %all-gather.19.cloned.1.call-start = ((), (), s32[]{:S(2)}) async-start(), calls=%async_computation.11 | async-start | bytes 7372800 | tf_op jit(solution)/shard_map/all_gather | solution.py:43
  137.7 23.3 %collective-permute-start = (f32[640,320]{0,1:T(8,128)}, f32[640,320]{0,1:T(8,128)}, u32[]{:S(2)}, u32[]{:S(2)}) collective-permute-start(f32[640,320]{0,1:T(8,128)} %param.12), channel_id=1, source_target_pairs={{0,8},{8,16},{16,24},{24,0},{1,9},{9,17},{17,25},{25,1},{2,10},{10... | collective-permute-start | bytes 2457608 | tf_op jit(solution)/shard_map/ppermute | solution.py:18
  139.2 38.1 %collective-permute-start.1 = (f32[640,320]{0,1:T(8,128)}, f32[640,320]{0,1:T(8,128)}, u32[]{:S(2)}, u32[]{:S(2)}) collective-permute-start(f32[640,320]{0,1:T(8,128)} %param.12), channel_id=1, source_target_pairs={{0,24},{8,0},{16,8},{24,16},{1,25},{9,1},{17,9},{25,17},{2,26},{10... | collective-permute-start | bytes 2457608 | tf_op jit(solution)/shard_map/ppermute | solution.py:21
  161.0 34.0 %collective-permute-start.2 = (f32[640,320]{0,1:T(8,128)}, f32[640,320]{0,1:T(8,128)}, u32[]{:S(2)}, u32[]{:S(2)}) collective-permute-start(f32[640,320]{0,1:T(8,128)} %collective-permute-done), channel_id=1, source_target_pairs={{0,8},{8,16},{16,24},{24,0},{1,9},{9,17},{17,25},{25,1},{2,10},{10... | collective-permute-start | bytes 2457608 | tf_op jit(solution)/shard_map/ppermute | solution.py:18
  249.0 135.6 %reduce-scatter.10.cloned.1.call-start = ((), (), s32[]{:S(2)}) async-start(), calls=%async_computation.12 | async-start | bytes 4915200 | tf_op jit(solution)/shard_map/reduce_scatter | solution.py:87
  311.7 151.2 %copy-start.2 = (f32[640,320]{0,1:T(8,128)S(1)}, f32[640,320]{0,1:T(8,128)}, u32[]{:S(2)}) copy-start(f32[640,320]{0,1:T(8,128)} %broadcast_multiply_fusion) | copy-start | bytes 2457604
  311.7 151.2 %all-gather.21.cloned.1.call-start = ((), (), s32[]{:S(2)}) async-start(), calls=%async_computation.13 | async-start | bytes 4915200 | tf_op jit(solution)/shard_map/all_gather | solution.py:90
  384.6 135.8 %all-gather.23.cloned.1.call-start = ((), (), s32[]{:S(2)}) async-start(), calls=%async_computation.14 | async-start | bytes 7372800 | tf_op jit(solution)/shard_map/all_gather | solution.py:43
  475.0 133.3 %reduce-scatter.12.cloned.1.call-start = ((), (), s32[]{:S(2)}) async-start(), calls=%async_computation.15 | async-start | bytes 4915200 | tf_op jit(solution)/shard_map/reduce_scatter | solution.py:87
  535.5 151.4 %copy-start.1 = (f32[640,320]{0,1:T(8,128)S(1)}, f32[640,320]{0,1:T(8,128)}, u32[]{:S(2)}) copy-start(f32[640,320]{0,1:T(8,128)} %multiply_subtract_fusion) | copy-start | bytes 2457604
  535.5 151.3 %all-gather.25.cloned.1.call-start = ((), (), s32[]{:S(2)}) async-start(), calls=%async_computation.16 | async-start | bytes 4915200 | tf_op jit(solution)/shard_map/all_gather | solution.py:90
  608.3 125.6 %all-gather.11.cloned.1.call-start = ((), (), s32[]{:S(2)}) async-start(), calls=%async_computation.5 | async-start | bytes 7372800 | tf_op jit(solution)/shard_map/all_gather | solution.py:43
  608.9 125.0 %copy-start.3 = (bf16[640,320]{0,1:T(8,128)(2,1)S(1)}, bf16[640,320]{0,1:T(8,128)(2,1)}, u32[]{:S(2)}) copy-start(bf16[640,320]{0,1:T(8,128)(2,1)} %param.9) | copy-start | bytes 1228804
  608.9 174.3 %all-gather.27.cloned.1.call-start = ((), (), s32[]{:S(2)}) async-start(), calls=%async_computation.17 | async-start | bytes 7372800 | tf_op jit(solution)/shard_map/all_gather | solution.py:43
  698.9 84.3 %copy-start = (f32[640,320]{0,1:T(8,128)S(1)}, f32[640,320]{0,1:T(8,128)}, u32[]{:S(2)}) copy-start(f32[640,320]{0,1:T(8,128)} %fusion.4) | copy-start | bytes 2457604
  698.9 148.9 %reduce-scatter.6.cloned.1.call-start = ((), (), s32[]{:S(2)}) async-start(), calls=%async_computation.6 | async-start | bytes 4096000 | tf_op jit(solution)/shard_map/reduce_scatter | solution.py:66
  745.3 177.7 %reduce-scatter.14.cloned.1.call-start = ((), (), s32[]{:S(2)}) async-start(), calls=%async_computation.18 | async-start | bytes 4915200 | tf_op jit(solution)/shard_map/reduce_scatter | solution.py:87
  798.1 49.8 %copy-start.4 = (f32[640,320]{0,1:T(8,128)S(1)}, f32[640,320]{0,1:T(8,128)}, u32[]{:S(2)}) copy-start(f32[640,320]{0,1:T(8,128)} %param.14) | copy-start | bytes 2457604
  798.1 49.8 %copy-start.5 = (f32[640,320]{0,1:T(8,128)S(1)}, f32[640,320]{0,1:T(8,128)}, u32[]{:S(2)}) copy-start(f32[640,320]{0,1:T(8,128)} %param.13) | copy-start | bytes 2457604
  798.1 125.0 %copy-start.7 = (f32[2,640]{1,0:T(2,128)S(1)}, f32[2,640]{1,0:T(2,128)}, u32[]{:S(2)}) copy-start(f32[2,640]{1,0:T(2,128)} %param.10) | copy-start | bytes 15364
  798.1 125.0 %copy-start.8 = (f32[2,640]{1,0:T(2,128)S(1)}, f32[2,640]{1,0:T(2,128)}, u32[]{:S(2)}) copy-start(f32[2,640]{1,0:T(2,128)} %param.15) | copy-start | bytes 15364
  798.1 125.0 %copy-start.9 = (f32[2,640]{1,0:T(2,128)S(1)}, f32[2,640]{1,0:T(2,128)}, u32[]{:S(2)}) copy-start(f32[2,640]{1,0:T(2,128)} %param.16) | copy-start | bytes 15364
  798.1 125.0 %copy-start.10 = (f32[2,640]{1,0:T(2,128)S(1)}, f32[2,640]{1,0:T(2,128)}, u32[]{:S(2)}) copy-start(f32[2,640]{1,0:T(2,128)} %param.17) | copy-start | bytes 15364
  798.1 193.0 %all-gather.13.cloned.1.call-start = ((), (), s32[]{:S(2)}) async-start(), calls=%async_computation.7 | async-start | bytes 4096000 | tf_op jit(solution)/shard_map/all_gather | solution.py:80
  850.6 217.2 %all-gather.29.cloned.1.call-start = ((), (), s32[]{:S(2)}) async-start(), calls=%async_computation.19 | async-start | bytes 4915200 | tf_op jit(solution)/shard_map/all_gather | solution.py:90
Sparse Core Ops, SparseCore 0:
  9.6 41.7 all-gather.14
  72.0 63.4 reduce-scatter.7
  138.1 46.6 all-gather.16
  249.1 47.4 all-gather.18
  311.9 72.6 reduce-scatter.9
  386.1 76.7 all-gather.20
  475.1 45.1 all-gather.22
  535.6 72.6 reduce-scatter.11
  610.0 76.7 all-gather.24
  688.7 45.1 all-gather.10
  736.6 46.6 all-gather.26
  785.5 62.2 reduce-scatter.5
  850.2 72.8 reduce-scatter.13
  925.2 65.9 all-gather.12
  992.7 75.0 all-gather.28
